TPU v7x, 256 devices: a whole 4x4x8 slice. The times are simulated.
256 devices in a mesh: dp: 4 (over y), ctx: 32 (over x_hi, z, core), head: 2 (over x_lo).
Axes of the slice: x: 4 (x_hi: 2, x_lo: 2; x = x_hi * 2 + x_lo), y: 4, z: 8, core: 2. Of those that a mesh axis runs over, the one named last changes fastest.
Arguments:
- queries: bfloat16 [4, 8192, 2048], P('dp', 'ctx', 'head'), may hold values from -35 to 35
- key_rows: bfloat16 [4, 8192, 2048], P('dp', 'ctx', 'head'), may hold values from -6 to 6
- value_rows: bfloat16 [4, 8192, 2048], P('dp', 'ctx', 'head'), may hold values from -6 to 6
- sink_logits: float32 [16], P('head'), may hold values from 4 to 9
- partner: int32 [3, 32], replicated, may hold values from 0 to 31, as said below
- block_pick: int32 [4, 3, 32], P('dp'), may hold values from 0 to 1
- out_grad: bfloat16 [4, 8192, 2048], P('dp', 'ctx', 'head'), may hold values from -18 to 18
Outputs:
- attention: bfloat16 [4, 8192, 2048], P('dp', 'ctx', 'head')
- query_grad: bfloat16 [4, 8192, 2048], P('dp', 'ctx', 'head')
- key_grad: bfloat16 [4, 8192, 2048], P('dp', 'ctx', 'head')
- value_grad: bfloat16 [4, 8192, 2048], P('dp', 'ctx', 'head')
- sink_grad: float32 [16], P('head')
Inputs may be any that keep to these rules, and one draw needn't show every extreme that they name: partner[r, i] = i XOR partner[r, 0] for every round r, and partner[r, 0] is a power of two: each round pairs the indices of ctx that differ in one bit.
All inputs are finite; a program needn't handle non-finite values.
Results may differ from a plain program's by a relative error of at most 0.0093.
Values may be sent and summed in bfloat16 or wider, within the bound.
No kernel may reach another device: no remote copies, remote signals or barrier semaphores. Data moves between devices by JAX's collectives and lax.ppermute only.
A program may use at most 128 MiB of HBM per device.

v0:
```python
import math
import jax
import jax.numpy as jnp
from jax import lax
from jax.sharding import PartitionSpec as P

HD = 128
BLOCK = 128
ROUNDS = 3


def partner_2(value, axis, apart):
    mask = 2**apart
    pairs = [(source, source ^ mask) for source in range(lax.axis_size(axis))]
    return lax.ppermute(value, axis, pairs)


def broadcast(value, axis, source):
    kept = jnp.where(lax.axis_index(axis) == source, value, 0).astype(value.dtype)
    return lax.psum(kept, axis)


def padded(shard, sides, width):
    for axis, dim in sides:
        peers, length = (lax.axis_size(axis), shard.shape[dim])
        up = [(i, (i + 1) % peers) for i in range(peers - 1)]
        down = [(j, i) for i, j in up]
        last = lax.slice_in_dim(shard, length - width, length, axis=dim)
        leading = lax.slice_in_dim(shard, 0, width, axis=dim)
        before = lax.ppermute(last, axis, up)
        after = lax.ppermute(leading, axis, down)
        shard = jnp.concatenate([before, shard, after], axis=dim)
    return shard


def passed_along(shard, axis, by):
    peers = lax.axis_size(axis)
    pairs = [(i, i + by) for i in range(peers) if 0 <= i + by < peers]
    return lax.ppermute(shard, axis, pairs)


def to_heads(matrix, head_count):
    return matrix.reshape(matrix.shape[0], head_count, HD).transpose(1, 0, 2)


def from_heads(tensor):
    return tensor.transpose(1, 0, 2).reshape(tensor.shape[1], tensor.shape[0] * tensor.shape[2])


def place_rows(piece, start, length_total):
    widths = [(0, 0)] * piece.ndim
    widths[piece.ndim - 2] = (start, length_total - start - piece.shape[-2])
    return jnp.pad(piece, widths)


def route_apart(package, xor_mask, bit_count):
    for bit_place in range(bit_count):
        arrived = partner_2(package, "ctx", bit_place)
        package = jnp.where(jnp.right_shift(xor_mask, bit_place) % 2 == 1, arrived, package)
    return package


def return_apart(package, xor_mask, bit_count):
    for bit_place in range(bit_count):
        arrived = partner_2(package, "ctx", bit_place)
        package = jnp.where(jnp.right_shift(xor_mask, bit_place) % 2 == 1, arrived, package)
    return package


def body(queries, key_rows, value_rows, sink_logits, partner, block_pick, out_grad):
    own_query = queries[0]
    own_keys = key_rows[0]
    own_values = value_rows[0]
    own_grad = out_grad[0]
    tokens = own_query.shape[0]
    feature_width = own_query.shape[1]
    head_count = feature_width // HD
    shard_blocks = tokens // BLOCK
    ctx_count = lax.axis_size("ctx")
    ctx_place = lax.axis_index("ctx")
    bit_count = ctx_count.bit_length() - 1
    scaling = HD ** (-0.5)
    is_first = ctx_place == 0
    is_last = ctx_place == ctx_count - 1
    slot_count = (5 + ROUNDS) * BLOCK
    first_pack = jnp.stack(
        [own_query[:BLOCK], own_keys[:BLOCK], own_values[:BLOCK], own_grad[:BLOCK]]
    )
    last_pack = jnp.stack(
        [
            own_query[tokens - BLOCK :],
            own_keys[tokens - BLOCK :],
            own_values[tokens - BLOCK :],
            own_grad[tokens - BLOCK :],
        ]
    )
    first_got = broadcast(first_pack, "ctx", 0)
    last_got = broadcast(last_pack, "ctx", ctx_count - 1)
    global_pack = jnp.concatenate([first_got, last_got], axis=1)
    global_query = to_heads(global_pack[0], head_count)
    global_grad = to_heads(global_pack[3], head_count)
    pair_rows = jnp.concatenate([own_keys, own_values], axis=1)
    extended = padded(pair_rows, (("ctx", 0),), BLOCK)
    xor_masks = partner[:, 0]
    partner_place = jnp.bitwise_xor(ctx_place, xor_masks)
    ctx_match = jnp.arange(ctx_count)[None, :] == partner_place[:, None]
    wanted = jnp.sum(jnp.where(ctx_match, block_pick[0], 0), axis=1)
    packages = jnp.stack(
        [
            lax.dynamic_slice_in_dim(pair_rows, wanted[number] * BLOCK, BLOCK, 0)
            for number in range(ROUNDS)
        ]
    )
    fetched = jnp.stack(
        [route_apart(packages[number], xor_masks[number], bit_count) for number in range(ROUNDS)]
    )
    global_pair = jnp.concatenate([global_pack[1], global_pack[2]], axis=1)
    shared_pair = jnp.concatenate(
        [global_pair, fetched.reshape(ROUNDS * BLOCK, 2 * feature_width)], axis=0
    )
    window_pair = jnp.stack(
        [
            extended[step * BLOCK : step * BLOCK + tokens].reshape(
                shard_blocks, BLOCK, 2 * feature_width
            )
            for step in range(3)
        ],
        axis=1,
    ).reshape(shard_blocks, 3 * BLOCK, 2 * feature_width)
    slot_pair = jnp.concatenate(
        [
            window_pair,
            jnp.broadcast_to(
                shared_pair[None], (shard_blocks, (2 + ROUNDS) * BLOCK, 2 * feature_width)
            ),
        ],
        axis=1,
    )
    slot_keys = (
        slot_pair[:, :, :feature_width]
        .reshape(shard_blocks, slot_count, head_count, HD)
        .transpose(2, 0, 1, 3)
    )
    slot_values = (
        slot_pair[:, :, feature_width:]
        .reshape(shard_blocks, slot_count, head_count, HD)
        .transpose(2, 0, 1, 3)
    )
    query_heads = to_heads(own_query, head_count)
    query_blocks = query_heads.reshape(head_count, shard_blocks, BLOCK, HD)
    key_heads = to_heads(own_keys, head_count)
    value_heads = to_heads(own_values, head_count)
    block_index = jnp.arange(shard_blocks)
    prev_ok = jnp.logical_not(is_first & (block_index == 1))
    next_ok = jnp.logical_not(is_last & (block_index == shard_blocks - 2))
    slot_valid = jnp.concatenate(
        [
            jnp.broadcast_to(prev_ok[:, None], (shard_blocks, BLOCK)),
            jnp.ones((shard_blocks, BLOCK), bool),
            jnp.broadcast_to(next_ok[:, None], (shard_blocks, BLOCK)),
            jnp.ones((shard_blocks, (2 + ROUNDS) * BLOCK), bool),
        ],
        axis=1,
    )
    sink_grid = sink_logits[:, None, None]
    scores = (
        jnp.einsum("hnqd,hnkd->hnqk", query_blocks, slot_keys, preferred_element_type=jnp.float32)
        * scaling
    )
    scores = jnp.where(slot_valid[None, :, None, :], scores, -jnp.inf)
    row_top = jnp.maximum(sink_grid, jnp.max(scores, axis=3))
    expo = jnp.exp(scores - row_top[..., None])
    row_total = jnp.exp(sink_grid - row_top) + jnp.sum(expo, axis=3)
    regular_acc = jnp.einsum(
        "hnqk,hnkd->hnqd",
        expo.astype(jnp.bfloat16),
        slot_values,
        preferred_element_type=jnp.float32,
    )
    regular_out = (regular_acc / row_total[..., None]).reshape(head_count, tokens, HD)
    regular_lse = (row_top + jnp.log(row_total)).reshape(head_count, tokens)
    global_scores = (
        jnp.einsum("hgd,htd->hgt", global_query, key_heads, preferred_element_type=jnp.float32)
        * scaling
    )
    local_top = jnp.max(global_scores, axis=2)
    global_top = jnp.maximum(lax.pmax(local_top, "ctx"), sink_logits[:, None])
    global_expo = jnp.exp(global_scores - global_top[..., None])
    part_total = jnp.sum(global_expo, axis=2)
    part_acc = jnp.einsum(
        "hgt,htd->hgd",
        global_expo.astype(jnp.bfloat16),
        value_heads,
        preferred_element_type=jnp.float32,
    )
    summed_total, summed_acc = lax.psum((part_total, part_acc), "ctx")
    global_total = jnp.exp(sink_logits[:, None] - global_top) + summed_total
    global_out = summed_acc / global_total[..., None]
    global_lse = global_top + jnp.log(global_total)
    row_index = jnp.arange(tokens)
    first_rows = is_first & (row_index < BLOCK)
    last_rows = is_last & (row_index >= tokens - BLOCK)
    regular_rows = jnp.logical_not(first_rows | last_rows)
    out_heads = jnp.where(
        first_rows[None, :, None],
        place_rows(global_out[:, :BLOCK], 0, tokens),
        jnp.where(
            last_rows[None, :, None],
            place_rows(global_out[:, BLOCK:], tokens - BLOCK, tokens),
            regular_out,
        ),
    )
    attention_half = out_heads.astype(jnp.bfloat16)
    lse_rows = jnp.where(
        first_rows[None, :],
        jnp.pad(global_lse[:, :BLOCK], ((0, 0), (0, tokens - BLOCK))),
        jnp.where(
            last_rows[None, :],
            jnp.pad(global_lse[:, BLOCK:], ((0, 0), (tokens - BLOCK, 0))),
            regular_lse,
        ),
    )
    grad_heads = to_heads(own_grad, head_count)
    row_delta = jnp.sum(grad_heads.astype(jnp.float32) * attention_half.astype(jnp.float32), axis=2)
    grad_regular = jnp.where(regular_rows[None, :, None], grad_heads, jnp.zeros_like(grad_heads))
    grad_blocks = grad_regular.reshape(head_count, shard_blocks, BLOCK, HD)
    delta_blocks = jnp.where(regular_rows[None, :], row_delta, 0.0).reshape(
        head_count, shard_blocks, BLOCK
    )
    lse_blocks = regular_lse.reshape(head_count, shard_blocks, BLOCK)
    probs = jnp.exp(scores - lse_blocks[..., None])
    prob_grad = jnp.einsum(
        "hnqd,hnkd->hnqk", grad_blocks, slot_values, preferred_element_type=jnp.float32
    )
    score_grad = (probs * (prob_grad - delta_blocks[..., None])).astype(jnp.bfloat16)
    prob_half = probs.astype(jnp.bfloat16)
    regular_dq = (
        jnp.einsum("hnqk,hnkd->hnqd", score_grad, slot_keys, preferred_element_type=jnp.float32)
        * scaling
    ).reshape(head_count, tokens, HD)
    slot_dk = (
        jnp.einsum("hnqk,hnqd->hnkd", score_grad, query_blocks, preferred_element_type=jnp.float32)
        * scaling
    )
    slot_dv = jnp.einsum(
        "hnqk,hnqd->hnkd", prob_half, grad_blocks, preferred_element_type=jnp.float32
    )
    slot_both = jnp.stack([slot_dk, slot_dv])
    window_lower = slot_both[:, :, :, :BLOCK].reshape(2, head_count, tokens, HD)
    window_self = slot_both[:, :, :, BLOCK : 2 * BLOCK].reshape(2, head_count, tokens, HD)
    window_upper = slot_both[:, :, :, 2 * BLOCK : 3 * BLOCK].reshape(2, head_count, tokens, HD)
    from_above = passed_along(window_lower[:, :, :BLOCK].astype(jnp.bfloat16), "ctx", -1).astype(
        jnp.float32
    )
    from_below = passed_along(window_upper[:, :, tokens - BLOCK :], "ctx", 1)
    key_pair = (
        window_self
        + jnp.concatenate([window_lower[:, :, BLOCK:], from_above], axis=2)
        + jnp.concatenate([from_below, window_upper[:, :, : tokens - BLOCK]], axis=2)
    )
    global_slots = jnp.sum(slot_both[:, :, :, 3 * BLOCK : 5 * BLOCK], axis=2)
    random_pack = (
        jnp.sum(
            slot_both[:, :, :, 5 * BLOCK :].reshape(2, head_count, shard_blocks, ROUNDS, BLOCK, HD),
            axis=2,
        )
        .transpose(2, 0, 1, 3, 4)
        .astype(jnp.bfloat16)
    )
    global_probs = jnp.exp(global_scores - global_lse[..., None])
    global_att = global_out.astype(jnp.bfloat16)
    global_delta = jnp.sum(global_grad.astype(jnp.float32) * global_att.astype(jnp.float32), axis=2)
    global_dp = jnp.einsum(
        "hgd,htd->hgt", global_grad, value_heads, preferred_element_type=jnp.float32
    )
    global_ds = (global_probs * (global_dp - global_delta[..., None])).astype(jnp.bfloat16)
    part_dq = (
        jnp.einsum("hgt,htd->hgd", global_ds, key_heads, preferred_element_type=jnp.float32)
        * scaling
    )
    owned_dk = (
        jnp.einsum("hgt,hgd->htd", global_ds, global_query, preferred_element_type=jnp.float32)
        * scaling
    )
    owned_dv = jnp.einsum(
        "hgt,hgd->htd",
        global_probs.astype(jnp.bfloat16),
        global_grad,
        preferred_element_type=jnp.float32,
    )
    key_pair = key_pair + jnp.stack([owned_dk, owned_dv])
    summed_dq, summed_slots = lax.psum((part_dq, global_slots), "ctx")
    key_pair = key_pair + is_first.astype(jnp.float32) * place_rows(
        summed_slots[:, :, :BLOCK], 0, tokens
    )
    key_pair = key_pair + is_last.astype(jnp.float32) * place_rows(
        summed_slots[:, :, BLOCK:], tokens - BLOCK, tokens
    )
    returned = jnp.stack(
        [
            return_apart(random_pack[number], xor_masks[number], bit_count)
            for number in range(ROUNDS)
        ]
    )
    block_match = (jnp.arange(shard_blocks)[None, :] == wanted[:, None]).astype(jnp.float32)
    random_add = jnp.einsum("rn,rchbd->chnbd", block_match, returned.astype(jnp.float32)).reshape(
        2, head_count, tokens, HD
    )
    key_pair = key_pair + random_add
    query_total = jnp.where(
        first_rows[None, :, None],
        place_rows(summed_dq[:, :BLOCK], 0, tokens),
        jnp.where(
            last_rows[None, :, None],
            place_rows(summed_dq[:, BLOCK:], tokens - BLOCK, tokens),
            regular_dq,
        ),
    )
    sink_part = -jnp.sum(jnp.exp(sink_logits[:, None] - lse_rows) * row_delta, axis=1)
    sink_total = lax.psum(sink_part, ("dp", "ctx"))
    sink_grad = sink_total / math.sqrt(lax.axis_size("dp") * ctx_count * tokens)
    attention = from_heads(attention_half)[None]
    query_grad = from_heads(query_total.astype(jnp.bfloat16))[None]
    key_grad = from_heads(key_pair[0].astype(jnp.bfloat16))[None]
    value_grad = from_heads(key_pair[1].astype(jnp.bfloat16))[None]
    return (attention, query_grad, key_grad, value_grad, sink_grad)


def solution(mesh):
    return jax.shard_map(
        body,
        mesh=mesh,
        in_specs=(
            P("dp", "ctx", "head"),
            P("dp", "ctx", "head"),
            P("dp", "ctx", "head"),
            P("head"),
            P(),
            P("dp", None, None),
            P("dp", "ctx", "head"),
        ),
        out_specs=(
            P("dp", "ctx", "head"),
            P("dp", "ctx", "head"),
            P("dp", "ctx", "head"),
            P("dp", "ctx", "head"),
            P("head"),
        ),
        check_vma=False,
    )
```

profile of v0, /device:TPU:1, one launch (start us, length us, event | category | flops | bytes accessed | tf_op | source)
XLA Modules:
  0.0 1673.2 jit_solution(2412980870164297198)
XLA Ops:
  15.1 5.0 collective-permute-start
  56.3 4.7 copy.136
  62.6 4.2 collective-permute-start.4
  66.8 18.6 %collective-permute-done.8 = bf16[128,2048]{1,0:T(8,128)(2,1)} collective-permute-done((bf16[128,2048]{1,0:T(8,128)(2,1)}, bf16[128,2048]{1,0:T(8,128)(2,1)}, u32[]{:S(2)}, u32[]{:S(2)}) %collective-permute-start.8) | collective-permute-done | bytes 524320 | tf_op jit(solution)/shard_map/ppermute | solution.py:15
  86.5 4.1 collective-permute-start.9
  90.6 8.0 collective-permute-done.13
  103.8 5.1 collective-permute-start.5
  108.9 51.2 %collective-permute-done.9 = bf16[128,2048]{1,0:T(8,128)(2,1)S(1)} collective-permute-done((bf16[128,2048]{1,0:T(8,128)(2,1)S(1)}, bf16[128,2048]{1,0:T(8,128)(2,1)S(1)}, u32[]{:S(2)}, u32[]{:S(2)}) %collective-permute-start.9) | collective-permute-done | bytes 524320 | tf_op jit(solution)/shard_map/ppermute | solution.py:15
  164.5 21.6 %collective-permute-done.14 = bf16[128,2048]{1,0:T(8,128)(2,1)S(1)} collective-permute-done((bf16[128,2048]{1,0:T(8,128)(2,1)S(1)}, bf16[128,2048]{1,0:T(8,128)(2,1)S(1)}, u32[]{:S(2)}, u32[]{:S(2)}) %collective-permute-start.14) | collective-permute-done | bytes 524320 | tf_op jit(solution)/shard_map/ppermute | solution.py:15
  190.6 183.5 %all-reduce.14.cloned.1.call-done = (bf16[4,128,1024]{1,2,0:T(8,128)(2,1)}, bf16[4,128,1024]{1,2,0:T(8,128)(2,1)}) async-done(((bf16[4,128,1024]{1,2,0:T(8,128)(2,1)}, bf16[4,128,1024]{1,2,0:T(8,128)(2,1)}), (bf16[4,128,1024]{1,2,0:T(8,128)(2,1)}, bf16[4,128,1024]{1,2,0:T(8,128)(2,1)})) %all-reduce.14.cloned.1.call-update) | async-done | bytes 2097168 | tf_op jit(solution)/shard_map/psum | solution.py:20
  380.7 66.2 %pmax.7 = f32[8,256]{1,0:T(8,128)S(1)} all-reduce(f32[8,256]{1,0:T(8,128)S(1)} %get-tuple-element.72), channel_id=1, replica_groups=mesh['dp'=4,'ctx'=32,'head'=2] {'ctx'}, use_global_device_ids=true, to_apply=%region_3.4 | all-reduce | flops 2048 | bytes 16384 | tf_op jit(solution)/shard_map/pmax | solution.py:187
  447.3 71.4 %psum.52 = f32[8,256]{1,0:T(8,128)S(1)} all-reduce(f32[8,256]{1,0:T(8,128)S(1)} %fusion.38), channel_id=1, replica_groups=mesh['dp'=4,'ctx'=32,'head'=2] {'ctx'}, use_global_device_ids=true, to_apply=%region_6.7 | all-reduce | flops 2048 | bytes 16384 | tf_op jit(solution)/shard_map/psum | solution.py:196
  529.0 9.0 collective-permute-done.6
  538.1 11.5 collective-permute-done.11
  549.7 11.9 collective-permute-done.16
  569.4 4.0 fusion.10
  573.4 6.5 copy.137
  586.3 4.5 fusion.28
  590.8 6.5 copy.139
  597.2 8.3 fusion.56
  605.6 182.0 %all-reduce.10.cloned.1.call-done = f32[8,256,128]{2,1,0:T(8,128)} async-done(((f32[8,256,128]{2,1,0:T(8,128)}), f32[8,256,128]{2,1,0:T(8,128)}) %all-reduce.10.cloned.1.call-update) | async-done | bytes 1048592 | tf_op jit(solution)/shard_map/psum | solution.py:196
  792.2 5.6 multiply_convert_fusion
  811.4 139.2 %all-reduce.15 = bf16[8,256,128]{2,1,0:T(8,128)(2,1)S(1)} all-reduce(f32[8,256,128]{2,1,0:T(8,128)} %convolution_multiply_fusion.2), channel_id=1, replica_groups=mesh['dp'=4,'ctx'=32,'head'=2] {'ctx'}, use_global_device_ids=true, to_apply=%region_11.12 | all-reduce | flops 262144 | bytes 1572864 | tf_op jit(solution)/shard_map/psum | solution.py:292
  951.1 6.2 collective-permute-start.19
  973.2 328.8 %psum.55 = f32[8]{0:T(128)S(1)} all-reduce(f32[8]{0:T(128)S(1)} %neg.3), channel_id=1, replica_groups=mesh['dp'=4,'ctx'=32,'head'=2] {'dp','ctx'}, use_global_device_ids=true, to_apply=%region_17.18 | all-reduce | flops 8 | bytes 64 | tf_op jit(solution)/shard_map/psum | solution.py:320
  1315.1 22.8 %collective-permute-done.25 = bf16[2,8,128,128]{3,2,1,0:T(8,128)(2,1)S(1)} collective-permute-done((bf16[2,8,128,128]{3,2,1,0:T(8,128)(2,1)}, bf16[2,8,128,128]{3,2,1,0:T(8,128)(2,1)S(1)}, u32[]{:S(2)}, u32[]{:S(2)}) %collective-permute-start.25) | collective-permute-done | bytes 524320 | tf_op jit(solution)/shard_map/ppermute | solution.py:15
  1339.8 78.2 %collective-permute-done.21 = bf16[2,8,128,128]{3,2,1,0:T(8,128)(2,1)S(1)} collective-permute-done((bf16[2,8,128,128]{3,2,1,0:T(8,128)(2,1)S(1)}, bf16[2,8,128,128]{3,2,1,0:T(8,128)(2,1)S(1)}, u32[]{:S(2)}, u32[]{:S(2)}) %collective-permute-start.21) | collective-permute-done | bytes 524320 | tf_op jit(solution)/shard_map/ppermute | solution.py:15
  1418.2 23.5 %collective-permute-done.31 = bf16[2,8,128,128]{3,2,1,0:T(8,128)(2,1)S(1)} collective-permute-done((bf16[2,8,128,128]{3,2,1,0:T(8,128)(2,1)S(1)}, bf16[2,8,128,128]{3,2,1,0:T(8,128)(2,1)S(1)}, u32[]{:S(2)}, u32[]{:S(2)}) %collective-permute-start.31) | collective-permute-done | bytes 524320 | tf_op jit(solution)/shard_map/ppermute | solution.py:15
  1441.8 12.2 collective-permute-done.26
  1454.4 26.7 %collective-permute-done.32 = bf16[2,8,128,128]{3,2,1,0:T(8,128)(2,1)S(1)} collective-permute-done((bf16[2,8,128,128]{3,2,1,0:T(8,128)(2,1)S(1)}, bf16[2,8,128,128]{3,2,1,0:T(8,128)(2,1)S(1)}, u32[]{:S(2)}, u32[]{:S(2)}) %collective-permute-start.32) | collective-permute-done | bytes 524320 | tf_op jit(solution)/shard_map/ppermute | solution.py:15
  1482.0 15.6 collective-permute-done.27
  1498.5 152.1 %all-reduce.12.cloned.1.call-done = f32[2,8,256,128]{3,2,1,0:T(8,128)} async-done(((f32[2,8,256,128]{3,2,1,0:T(8,128)}), f32[2,8,256,128]{3,2,1,0:T(8,128)}) %all-reduce.12.cloned.1.call-update) | async-done | bytes 2097168 | tf_op jit(solution)/shard_map/psum | solution.py:292
  (259 shorter events, 148.0 us)
Async XLA Ops:
  7.2 366.9 %all-reduce.14.cloned.1.call-start = ((), (), s32[]{:S(2)}) async-start(), calls=%async_computation.2 | async-start | bytes 4194304 | tf_op jit(solution)/shard_map/psum | solution.py:20
  15.1 38.1 %collective-permute-start = (bf16[128,2048]{1,0:T(8,128)(2,1)}, bf16[128,2048]{1,0:T(8,128)(2,1)}, u32[]{:S(2)}, u32[]{:S(2)}) collective-permute-start(bf16[128,2048]{1,0:T(8,128)(2,1)} %get-tuple-element.51), channel_id=1, source_target_pairs={{0,2},{2,4},{4,6},{6,8},{8,10},{10,12},{12,14},{14,16},{16,18},{18... | collective-permute-start | bytes 1572872 | tf_op jit(solution)/shard_map/ppermute | solution.py:30
  20.1 33.1 %collective-permute-start.1 = (bf16[128,2048]{1,0:T(8,128)(2,1)}, bf16[128,2048]{1,0:T(8,128)(2,1)}, u32[]{:S(2)}, u32[]{:S(2)}) collective-permute-start(bf16[128,2048]{1,0:T(8,128)(2,1)} %get-tuple-element.52), channel_id=1, source_target_pairs={{2,0},{4,2},{6,4},{8,6},{10,8},{12,10},{14,12},{16,14},{18,16},{20... | collective-permute-start | bytes 1572872 | tf_op jit(solution)/shard_map/ppermute | solution.py:31
  22.3 22.2 %collective-permute-start.2 = (bf16[128,2048]{1,0:T(8,128)(2,1)}, bf16[128,2048]{1,0:T(8,128)(2,1)}, u32[]{:S(2)}, u32[]{:S(2)}) collective-permute-start(bf16[128,2048]{1,0:T(8,128)(2,1)} %get-tuple-element.53), channel_id=1, source_target_pairs={{0,2},{2,0},{4,6},{6,4},{8,10},{10,8},{12,14},{14,12},{16,18},{18,... | collective-permute-start | bytes 1572872 | tf_op jit(solution)/shard_map/ppermute | solution.py:15
  22.4 25.5 %collective-permute-start.7 = (bf16[128,2048]{1,0:T(8,128)(2,1)}, bf16[128,2048]{1,0:T(8,128)(2,1)}, u32[]{:S(2)}, u32[]{:S(2)}) collective-permute-start(bf16[128,2048]{1,0:T(8,128)(2,1)} %get-tuple-element.54), channel_id=1, source_target_pairs={{0,2},{2,0},{4,6},{6,4},{8,10},{10,8},{12,14},{14,12},{16,18},{18,... | collective-permute-start | bytes 1572872 | tf_op jit(solution)/shard_map/ppermute | solution.py:15
  22.9 26.9 %collective-permute-start.12 = (bf16[128,2048]{1,0:T(8,128)(2,1)}, bf16[128,2048]{1,0:T(8,128)(2,1)}, u32[]{:S(2)}, u32[]{:S(2)}) collective-permute-start(bf16[128,2048]{1,0:T(8,128)(2,1)} %get-tuple-element.55), channel_id=1, source_target_pairs={{0,2},{2,0},{4,6},{6,4},{8,10},{10,8},{12,14},{14,12},{16,18},{18,... | collective-permute-start | bytes 1572872 | tf_op jit(solution)/shard_map/ppermute | solution.py:15
  30.4 757.2 %all-reduce.10.cloned.1.call-start = ((), (), s32[]{:S(2)}) async-start(), calls=%async_computation | async-start | bytes 2097152 | tf_op jit(solution)/shard_map/psum | solution.py:196
  49.8 35.6 %collective-permute-start.8 = (bf16[128,2048]{1,0:T(8,128)(2,1)}, bf16[128,2048]{1,0:T(8,128)(2,1)}, u32[]{:S(2)}, u32[]{:S(2)}) collective-permute-start(bf16[128,2048]{1,0:T(8,128)(2,1)} %broadcast_select_fusion.16), channel_id=1, source_target_pairs={{0,4},{2,6},{4,0},{6,2},{8,12},{10,14},{12,8},{14,10},{16,20},{18,... | collective-permute-start | bytes 1572872 | tf_op jit(solution)/shard_map/ppermute | solution.py:15
  51.7 47.0 %collective-permute-start.13 = (bf16[128,2048]{1,0:T(8,128)(2,1)}, bf16[128,2048]{1,0:T(8,128)(2,1)}, u32[]{:S(2)}, u32[]{:S(2)}) collective-permute-start(bf16[128,2048]{1,0:T(8,128)(2,1)} %broadcast_select_fusion.12), channel_id=1, source_target_pairs={{0,4},{2,6},{4,0},{6,2},{8,12},{10,14},{12,8},{14,10},{16,20},{18,... | collective-permute-start | bytes 1572872 | tf_op jit(solution)/shard_map/ppermute | solution.py:15
  62.6 40.4 %collective-permute-start.4 = (bf16[128,2048]{1,0:T(8,128)(2,1)S(1)}, bf16[128,2048]{1,0:T(8,128)(2,1)S(1)}, u32[]{:S(2)}, u32[]{:S(2)}) collective-permute-start(bf16[128,2048]{1,0:T(8,128)(2,1)S(1)} %broadcast_select_fusion.21), channel_id=1, source_target_pairs={{0,8},{2,10},{4,12},{6,14},{8,0},{10,2},{12,4},{14,6},{16,24},{18,... | collective-permute-start | bytes 1572872 | tf_op jit(solution)/shard_map/ppermute | solution.py:15
  86.5 73.6 %collective-permute-start.9 = (bf16[128,2048]{1,0:T(8,128)(2,1)S(1)}, bf16[128,2048]{1,0:T(8,128)(2,1)S(1)}, u32[]{:S(2)}, u32[]{:S(2)}) collective-permute-start(bf16[128,2048]{1,0:T(8,128)(2,1)S(1)} %broadcast_select_fusion.17), channel_id=1, source_target_pairs={{0,8},{2,10},{4,12},{6,14},{8,0},{10,2},{12,4},{14,6},{16,24},{18,... | collective-permute-start | bytes 1572872 | tf_op jit(solution)/shard_map/ppermute | solution.py:15
  99.7 86.3 %collective-permute-start.14 = (bf16[128,2048]{1,0:T(8,128)(2,1)S(1)}, bf16[128,2048]{1,0:T(8,128)(2,1)S(1)}, u32[]{:S(2)}, u32[]{:S(2)}) collective-permute-start(bf16[128,2048]{1,0:T(8,128)(2,1)S(1)} %broadcast_select_fusion.13), channel_id=1, source_target_pairs={{0,8},{2,10},{4,12},{6,14},{8,0},{10,2},{12,4},{14,6},{16,24},{18,... | collective-permute-start | bytes 1572872 | tf_op jit(solution)/shard_map/ppermute | solution.py:15
  103.8 418.3 %collective-permute-start.5 = (bf16[128,2048]{1,0:T(8,128)(2,1)}, bf16[128,2048]{1,0:T(8,128)(2,1)}, u32[]{:S(2)}, u32[]{:S(2)}) collective-permute-start(bf16[128,2048]{1,0:T(8,128)(2,1)} %broadcast_select_fusion.22), channel_id=1, source_target_pairs={{0,16},{2,18},{4,20},{6,22},{8,24},{10,26},{12,28},{14,30},{16,0},... | collective-permute-start | bytes 1572872 | tf_op jit(solution)/shard_map/ppermute | solution.py:15
  161.0 362.7 %collective-permute-start.10 = (bf16[128,2048]{1,0:T(8,128)(2,1)}, bf16[128,2048]{1,0:T(8,128)(2,1)}, u32[]{:S(2)}, u32[]{:S(2)}) collective-permute-start(bf16[128,2048]{1,0:T(8,128)(2,1)} %broadcast_select_fusion.18), channel_id=1, source_target_pairs={{0,16},{2,18},{4,20},{6,22},{8,24},{10,26},{12,28},{14,30},{16,0},... | collective-permute-start | bytes 1572872 | tf_op jit(solution)/shard_map/ppermute | solution.py:15
  186.9 340.6 %collective-permute-start.15 = (bf16[128,2048]{1,0:T(8,128)(2,1)}, bf16[128,2048]{1,0:T(8,128)(2,1)}, u32[]{:S(2)}, u32[]{:S(2)}) collective-permute-start(bf16[128,2048]{1,0:T(8,128)(2,1)} %broadcast_select_fusion.14), channel_id=1, source_target_pairs={{0,16},{2,18},{4,20},{6,22},{8,24},{10,26},{12,28},{14,30},{16,0},... | collective-permute-start | bytes 1572872 | tf_op jit(solution)/shard_map/ppermute | solution.py:15
  522.0 1128.5 %all-reduce.12.cloned.1.call-start = ((), (), s32[]{:S(2)}) async-start(), calls=%async_computation.1 | async-start | bytes 4194304 | tf_op jit(solution)/shard_map/psum | solution.py:292
  524.8 24.8 %collective-permute-start.11 = (bf16[128,2048]{1,0:T(8,128)(2,1)S(1)}, bf16[128,2048]{1,0:T(8,128)(2,1)S(1)}, u32[]{:S(2)}, u32[]{:S(2)}) collective-permute-start(bf16[128,2048]{1,0:T(8,128)(2,1)S(1)} %broadcast_select_fusion.19), channel_id=1, source_target_pairs={{0,32},{2,34},{4,36},{6,38},{8,40},{10,42},{12,44},{14,46},{16,48}... | collective-permute-start | bytes 1572872 | tf_op jit(solution)/shard_map/ppermute | solution.py:15
  528.7 32.9 %collective-permute-start.16 = (bf16[128,2048]{1,0:T(8,128)(2,1)S(1)}, bf16[128,2048]{1,0:T(8,128)(2,1)S(1)}, u32[]{:S(2)}, u32[]{:S(2)}) collective-permute-start(bf16[128,2048]{1,0:T(8,128)(2,1)S(1)} %broadcast_select_fusion.15), channel_id=1, source_target_pairs={{0,32},{2,34},{4,36},{6,38},{8,40},{10,42},{12,44},{14,46},{16,48}... | collective-permute-start | bytes 1572872 | tf_op jit(solution)/shard_map/ppermute | solution.py:15
  959.9 349.2 %collective-permute-start.17 = (bf16[2,8,128,128]{3,2,1,0:T(8,128)(2,1)}, bf16[2,8,128,128]{3,2,1,0:T(8,128)(2,1)}, u32[]{:S(2)}, u32[]{:S(2)}) collective-permute-start(bf16[2,8,128,128]{3,2,1,0:T(8,128)(2,1)} %slice.260), channel_id=1, source_target_pairs={{2,0},{4,2},{6,4},{8,6},{10,8},{12,10},{14,12},{16,14},{18,16},{20... | collective-permute-start | bytes 1572872 | tf_op jit(solution)/shard_map/ppermute | solution.py:39
  968.6 341.6 %collective-permute-start.20 = (bf16[2,8,128,128]{3,2,1,0:T(8,128)(2,1)}, bf16[2,8,128,128]{3,2,1,0:T(8,128)(2,1)}, u32[]{:S(2)}, u32[]{:S(2)}) collective-permute-start(bf16[2,8,128,128]{3,2,1,0:T(8,128)(2,1)} %get-tuple-element.41), channel_id=1, source_target_pairs={{0,4},{2,6},{4,0},{6,2},{8,12},{10,14},{12,8},{14,10},{16,20},{18,... | collective-permute-start | bytes 1572872 | tf_op jit(solution)/shard_map/ppermute | solution.py:15
  970.1 341.5 %collective-permute-start.30 = (bf16[2,8,128,128]{3,2,1,0:T(8,128)(2,1)}, bf16[2,8,128,128]{3,2,1,0:T(8,128)(2,1)}, u32[]{:S(2)}, u32[]{:S(2)}) collective-permute-start(bf16[2,8,128,128]{3,2,1,0:T(8,128)(2,1)} %get-tuple-element.42), channel_id=1, source_target_pairs={{0,4},{2,6},{4,0},{6,2},{8,12},{10,14},{12,8},{14,10},{16,20},{18,... | collective-permute-start | bytes 1572872 | tf_op jit(solution)/shard_map/ppermute | solution.py:15
  1306.6 353.3 %collective-permute-start.18 = (f32[2,8,128,128]{3,2,1,0:T(8,128)}, f32[2,8,128,128]{3,2,1,0:T(8,128)}, u32[]{:S(2)}, u32[]{:S(2)}) collective-permute-start(f32[2,8,128,128]{3,2,1,0:T(8,128)} %get-tuple-element.35), channel_id=1, source_target_pairs={{0,2},{2,4},{4,6},{6,8},{8,10},{10,12},{12,14},{14,16},{16,18},{18... | collective-permute-start | bytes 3145736 | tf_op jit(solution)/shard_map/ppermute | solution.py:39
  1309.0 28.9 %collective-permute-start.25 = (bf16[2,8,128,128]{3,2,1,0:T(8,128)(2,1)}, bf16[2,8,128,128]{3,2,1,0:T(8,128)(2,1)S(1)}, u32[]{:S(2)}, u32[]{:S(2)}) collective-permute-start(bf16[2,8,128,128]{3,2,1,0:T(8,128)(2,1)} %get-tuple-element.43), channel_id=1, source_target_pairs={{0,4},{2,6},{4,0},{6,2},{8,12},{10,14},{12,8},{14,10},{16,20},{18,... | collective-permute-start | bytes 1572872 | tf_op jit(solution)/shard_map/ppermute | solution.py:15
  1311.3 106.7 %collective-permute-start.21 = (bf16[2,8,128,128]{3,2,1,0:T(8,128)(2,1)S(1)}, bf16[2,8,128,128]{3,2,1,0:T(8,128)(2,1)S(1)}, u32[]{:S(2)}, u32[]{:S(2)}) collective-permute-start(bf16[2,8,128,128]{3,2,1,0:T(8,128)(2,1)S(1)} %broadcast_select_fusion.9), channel_id=1, source_target_pairs={{0,8},{2,10},{4,12},{6,14},{8,0},{10,2},{12,4},{14,6},{16,24},{18,... | collective-permute-start | bytes 1572872 | tf_op jit(solution)/shard_map/ppermute | solution.py:15
  1312.7 129.0 %collective-permute-start.31 = (bf16[2,8,128,128]{3,2,1,0:T(8,128)(2,1)S(1)}, bf16[2,8,128,128]{3,2,1,0:T(8,128)(2,1)S(1)}, u32[]{:S(2)}, u32[]{:S(2)}) collective-permute-start(bf16[2,8,128,128]{3,2,1,0:T(8,128)(2,1)S(1)} %broadcast_select_fusion.1), channel_id=1, source_target_pairs={{0,8},{2,10},{4,12},{6,14},{8,0},{10,2},{12,4},{14,6},{16,24},{18,... | collective-permute-start | bytes 1572872 | tf_op jit(solution)/shard_map/ppermute | solution.py:15
  1339.0 115.0 %collective-permute-start.26 = (bf16[2,8,128,128]{3,2,1,0:T(8,128)(2,1)S(1)}, bf16[2,8,128,128]{3,2,1,0:T(8,128)(2,1)S(1)}, u32[]{:S(2)}, u32[]{:S(2)}) collective-permute-start(bf16[2,8,128,128]{3,2,1,0:T(8,128)(2,1)S(1)} %broadcast_select_fusion.5), channel_id=1, source_target_pairs={{0,8},{2,10},{4,12},{6,14},{8,0},{10,2},{12,4},{14,6},{16,24},{18,... | collective-permute-start | bytes 1572872 | tf_op jit(solution)/shard_map/ppermute | solution.py:15
  1418.1 36.1 %collective-permute-start.22 = (bf16[2,8,128,128]{3,2,1,0:T(8,128)(2,1)S(1)}, bf16[2,8,128,128]{3,2,1,0:T(8,128)(2,1)S(1)}, u32[]{:S(2)}, u32[]{:S(2)}) collective-permute-start(bf16[2,8,128,128]{3,2,1,0:T(8,128)(2,1)S(1)} %broadcast_select_fusion.10), channel_id=1, source_target_pairs={{0,16},{2,18},{4,20},{6,22},{8,24},{10,26},{12,28},{14,30},{16,0},... | collective-permute-start | bytes 1572872 | tf_op jit(solution)/shard_map/ppermute | solution.py:15
  1441.7 39.4 %collective-permute-start.32 = (bf16[2,8,128,128]{3,2,1,0:T(8,128)(2,1)S(1)}, bf16[2,8,128,128]{3,2,1,0:T(8,128)(2,1)S(1)}, u32[]{:S(2)}, u32[]{:S(2)}) collective-permute-start(bf16[2,8,128,128]{3,2,1,0:T(8,128)(2,1)S(1)} %broadcast_select_fusion.2), channel_id=1, source_target_pairs={{0,16},{2,18},{4,20},{6,22},{8,24},{10,26},{12,28},{14,30},{16,0},... | collective-permute-start | bytes 1572872 | tf_op jit(solution)/shard_map/ppermute | solution.py:15
  1454.1 43.5 %collective-permute-start.27 = (bf16[2,8,128,128]{3,2,1,0:T(8,128)(2,1)S(1)}, bf16[2,8,128,128]{3,2,1,0:T(8,128)(2,1)S(1)}, u32[]{:S(2)}, u32[]{:S(2)}) collective-permute-start(bf16[2,8,128,128]{3,2,1,0:T(8,128)(2,1)S(1)} %broadcast_select_fusion.6), channel_id=1, source_target_pairs={{0,16},{2,18},{4,20},{6,22},{8,24},{10,26},{12,28},{14,30},{16,0},... | collective-permute-start | bytes 1572872 | tf_op jit(solution)/shard_map/ppermute | solution.py:15
  1454.3 196.3 %collective-permute-start.23 = (bf16[2,8,128,128]{3,2,1,0:T(8,128)(2,1)S(1)}, bf16[2,8,128,128]{3,2,1,0:T(8,128)(2,1)}, u32[]{:S(2)}, u32[]{:S(2)}) collective-permute-start(bf16[2,8,128,128]{3,2,1,0:T(8,128)(2,1)S(1)} %broadcast_select_fusion.11), channel_id=1, source_target_pairs={{0,32},{2,34},{4,36},{6,38},{8,40},{10,42},{12,44},{14,46},{16,48}... | collective-permute-start | bytes 1572872 | tf_op jit(solution)/shard_map/ppermute | solution.py:15
  1482.0 169.6 %collective-permute-start.33 = (bf16[2,8,128,128]{3,2,1,0:T(8,128)(2,1)}, bf16[2,8,128,128]{3,2,1,0:T(8,128)(2,1)}, u32[]{:S(2)}, u32[]{:S(2)}) collective-permute-start(bf16[2,8,128,128]{3,2,1,0:T(8,128)(2,1)} %broadcast_select_fusion.3), channel_id=1, source_target_pairs={{0,32},{2,34},{4,36},{6,38},{8,40},{10,42},{12,44},{14,46},{16,48}... | collective-permute-start | bytes 1572872 | tf_op jit(solution)/shard_map/ppermute | solution.py:15
  1498.5 155.3 %collective-permute-start.28 = (bf16[2,8,128,128]{3,2,1,0:T(8,128)(2,1)}, bf16[2,8,128,128]{3,2,1,0:T(8,128)(2,1)}, u32[]{:S(2)}, u32[]{:S(2)}) collective-permute-start(bf16[2,8,128,128]{3,2,1,0:T(8,128)(2,1)} %broadcast_select_fusion.7), channel_id=1, source_target_pairs={{0,32},{2,34},{4,36},{6,38},{8,40},{10,42},{12,44},{14,46},{16,48}... | collective-permute-start | bytes 1572872 | tf_op jit(solution)/shard_map/ppermute | solution.py:15
  (44 other events, 2210.3 us)
Sparse Core Ops, SparseCore 0:
  30.5 343.5 all-reduce.13
  522.2 265.3 all-reduce.9
  1306.7 343.7 all-reduce.11
where the time goes:
time: 1680 us; the launch traced here: 1670 us
  waiting for transfers between devices  829 us (49%)
  blocking collectives  606 us (36%)
  other arithmetic  61.1 us (4%)
  local copies, waits for them, and re-layouts  59.5 us (4%)
  starting transfers between devices  54.6 us (3%)
  matrix products  36.7 us (2%)
  between operations  26.6 us (2%)
    psum x1, blocking collectives, body(): sink_total = lax.psum(sink_part, ('dp', 'ctx'))  329 us
    ppermute x30, waiting for transfers between devices, partner_2(): return lax.ppermute(value, axis, pairs)  311 us
    psum x1, waiting for transfers between devices, broadcast(): return lax.psum(kept, axis)  183 us
    psum x1, waiting for transfers between devices, body(): summed_total, summed_acc = lax.psum((part_total, part_acc), 'ctx')  182 us
    psum x1, waiting for transfers between devices, body(): summed_dq, summed_slots = lax.psum((part_dq, global_slots), 'ctx')  152 us
    psum x1, blocking collectives, body(): summed_dq, summed_slots = lax.psum((part_dq, global_slots), 'ctx')  139 us
    psum x1, blocking collectives, body(): summed_total, summed_acc = lax.psum((part_total, part_acc), 'ctx')  71.4 us
    pmax x1, blocking collectives, body(): global_top = jnp.maximum(lax.pmax(local_top, 'ctx'), sink_logits[:, None])  66.2 us
  transfers between devices with their start and end apart: 37, of which 17 were waited for; matrix products, arithmetic and copies ran while one was open for 7% of the time, Pallas kernels for 0%

commit v1 on v0

--- a/solution.py
+++ b/solution.py
@@ -317,7 +317,7 @@
         ),
     )
     sink_part = -jnp.sum(jnp.exp(sink_logits[:, None] - lse_rows) * row_delta, axis=1)
-    sink_total = lax.psum(sink_part, ("dp", "ctx"))
+    sink_total = lax.psum(lax.psum(sink_part, "ctx"), "dp")
     sink_grad = sink_total / math.sqrt(lax.axis_size("dp") * ctx_count * tokens)
     attention = from_heads(attention_half)[None]
     query_grad = from_heads(query_total.astype(jnp.bfloat16))[None]

time: 1680 us -> 1390 us (0.83)
  blocking collectives: 606 us -> 287 us
    psum x1, blocking collectives: 329 us -> 8.42 us  [body(): sink_total = lax.psum(lax.psum(sink_part, 'ctx'), 'dp')]
    psum x1, waiting for transfers between devices: 152 us -> 239 us  [body(): summed_dq, summed_slots = lax.psum((part_dq, global_slots), 'ctx')]
    ppermute x30, waiting for transfers between devices: 311 us -> 240 us  [partner_2(): return lax.ppermute(value, axis, pairs)]
  transfers between devices with their start and end apart: 37 -> 37, of which waited for: 17 -> 18; matrix products, arithmetic and copies ran while one was open for 7% -> 9% of each run, Pallas kernels for 0% -> 0%
where the time goes in v1:
time: 1390 us; the launch traced here: 1380 us
  waiting for transfers between devices  844 us (61%)
  blocking collectives  287 us (21%)
  starting transfers between devices  68.4 us (5%)
  other arithmetic  61.2 us (4%)
  local copies, waits for them, and re-layouts  60.5 us (4%)
  matrix products  36.7 us (3%)
  between operations  26.6 us (2%)
    ppermute x30, waiting for transfers between devices, partner_2(): return lax.ppermute(value, axis, pairs)  240 us
    psum x1, waiting for transfers between devices, body(): summed_dq, summed_slots = lax.psum((part_dq, global_slots), 'ctx')  239 us
    psum x1, waiting for transfers between devices, broadcast(): return lax.psum(kept, axis)  183 us
    psum x1, waiting for transfers between devices, body(): summed_total, summed_acc = lax.psum((part_total, part_acc), 'ctx')  182 us
    psum x1, blocking collectives, body(): summed_dq, summed_slots = lax.psum((part_dq, global_slots), 'ctx')  141 us
    psum x1, blocking collectives, body(): summed_total, summed_acc = lax.psum((part_total, part_acc), 'ctx')  71.4 us
    pmax x1, blocking collectives, body(): global_top = jnp.maximum(lax.pmax(local_top, 'ctx'), sink_logits[:, None])  66.2 us
    ppermute x30, starting transfers between devices, partner_2(): return lax.ppermute(value, axis, pairs)  53 us
  transfers between devices with their start and end apart: 37, of which 18 were waited for; matrix products, arithmetic and copies ran while one was open for 9% of the time, Pallas kernels for 0%

profile of v1, /device:TPU:1, one launch (start us, length us, event | category | flops | bytes accessed | tf_op | source)
XLA Modules:
  0.0 1384.8 jit_solution(13068888172570105390)
XLA Ops:
  15.0 5.0 collective-permute-start
  56.3 4.7 copy.136
  66.8 18.5 %collective-permute-done.8 = bf16[128,2048]{1,0:T(8,128)(2,1)} collective-permute-done((bf16[128,2048]{1,0:T(8,128)(2,1)}, bf16[128,2048]{1,0:T(8,128)(2,1)}, u32[]{:S(2)}, u32[]{:S(2)}) %collective-permute-start.8) | collective-permute-done | bytes 524320 | tf_op jit(solution)/shard_map/ppermute | solution.py:15
  90.5 8.0 collective-permute-done.13
  103.8 5.1 collective-permute-start.5
  108.9 51.2 %collective-permute-done.9 = bf16[128,2048]{1,0:T(8,128)(2,1)S(1)} collective-permute-done((bf16[128,2048]{1,0:T(8,128)(2,1)S(1)}, bf16[128,2048]{1,0:T(8,128)(2,1)S(1)}, u32[]{:S(2)}, u32[]{:S(2)}) %collective-permute-start.9) | collective-permute-done | bytes 524320 | tf_op jit(solution)/shard_map/ppermute | solution.py:15
  164.5 21.5 %collective-permute-done.14 = bf16[128,2048]{1,0:T(8,128)(2,1)S(1)} collective-permute-done((bf16[128,2048]{1,0:T(8,128)(2,1)S(1)}, bf16[128,2048]{1,0:T(8,128)(2,1)S(1)}, u32[]{:S(2)}, u32[]{:S(2)}) %collective-permute-start.14) | collective-permute-done | bytes 524320 | tf_op jit(solution)/shard_map/ppermute | solution.py:15
  190.6 182.8 %all-reduce.15.cloned.1.call-done = (bf16[4,128,1024]{1,2,0:T(8,128)(2,1)}, bf16[4,128,1024]{1,2,0:T(8,128)(2,1)}) async-done(((bf16[4,128,1024]{1,2,0:T(8,128)(2,1)}, bf16[4,128,1024]{1,2,0:T(8,128)(2,1)}), (bf16[4,128,1024]{1,2,0:T(8,128)(2,1)}, bf16[4,128,1024]{1,2,0:T(8,128)(2,1)})) %all-reduce.15.cloned.1.call-update) | async-done | bytes 2097168 | tf_op jit(solution)/shard_map/psum | solution.py:20
  380.1 66.2 %pmax.7 = f32[8,256]{1,0:T(8,128)S(1)} all-reduce(f32[8,256]{1,0:T(8,128)S(1)} %get-tuple-element.74), channel_id=1, replica_groups=mesh['dp'=4,'ctx'=32,'head'=2] {'ctx'}, use_global_device_ids=true, to_apply=%region_3.4 | all-reduce | flops 2048 | bytes 16384 | tf_op jit(solution)/shard_map/pmax | solution.py:187
  446.6 71.4 %psum.59 = f32[8,256]{1,0:T(8,128)S(1)} all-reduce(f32[8,256]{1,0:T(8,128)S(1)} %fusion.38), channel_id=1, replica_groups=mesh['dp'=4,'ctx'=32,'head'=2] {'ctx'}, use_global_device_ids=true, to_apply=%region_6.7 | all-reduce | flops 2048 | bytes 16384 | tf_op jit(solution)/shard_map/psum | solution.py:196
  528.4 9.0 collective-permute-done.6
  537.5 11.5 collective-permute-done.11
  549.1 11.9 collective-permute-done.16
  572.8 6.5 copy.137
  585.8 4.5 fusion.28
  590.3 6.5 copy.139
  596.7 8.4 fusion.56
  605.1 181.8 %all-reduce.11.cloned.1.call-done = f32[8,256,128]{2,1,0:T(8,128)} async-done(((f32[8,256,128]{2,1,0:T(8,128)}), f32[8,256,128]{2,1,0:T(8,128)}) %all-reduce.11.cloned.1.call-update) | async-done | bytes 1048592 | tf_op jit(solution)/shard_map/psum | solution.py:196
  791.6 5.6 multiply_convert_fusion
  811.0 141.2 %all-reduce.16 = (bf16[8,256,128]{2,1,0:T(8,128)(2,1)}, f32[8]{0:T(128)S(1)}) all-reduce(f32[8,256,128]{2,1,0:T(8,128)} %convolution_multiply_fusion.2, f32[8]{0:T(128)S(1)} %neg.3), channel_id=1, replica_groups=mesh['dp'=4,'ctx'=32,'head'=2] {'ctx'}, use_global_device_ids=true, to_apply=%region_11.12 | all-reduce | flops 262152 | bytes 1572928 | tf_op jit(solution)/shard_map/psum | solution.py:292
  953.5 6.2 collective-permute-start.19
  975.7 8.4 psum.63
  988.7 5.8 collective-permute-start.18
  1001.1 29.7 %collective-permute-done.25 = bf16[2,8,128,128]{3,2,1,0:T(8,128)(2,1)S(1)} collective-permute-done((bf16[2,8,128,128]{3,2,1,0:T(8,128)(2,1)}, bf16[2,8,128,128]{3,2,1,0:T(8,128)(2,1)S(1)}, u32[]{:S(2)}, u32[]{:S(2)}) %collective-permute-start.25) | collective-permute-done | bytes 524320 | tf_op jit(solution)/shard_map/ppermute | solution.py:15
  1032.4 14.9 %collective-permute-done.21 = bf16[2,8,128,128]{3,2,1,0:T(8,128)(2,1)S(1)} collective-permute-done((bf16[2,8,128,128]{3,2,1,0:T(8,128)(2,1)S(1)}, bf16[2,8,128,128]{3,2,1,0:T(8,128)(2,1)S(1)}, u32[]{:S(2)}, u32[]{:S(2)}) %collective-permute-start.21) | collective-permute-done | bytes 524320 | tf_op jit(solution)/shard_map/ppermute | solution.py:15
  1047.3 6.8 collective-permute-start.22
  1054.1 11.3 collective-permute-done.31
  1068.9 12.1 collective-permute-done.26
  1081.2 12.1 collective-permute-done.22
  1093.4 21.4 %collective-permute-done.32 = bf16[2,8,128,128]{3,2,1,0:T(8,128)(2,1)S(1)} collective-permute-done((bf16[2,8,128,128]{3,2,1,0:T(8,128)(2,1)S(1)}, bf16[2,8,128,128]{3,2,1,0:T(8,128)(2,1)S(1)}, u32[]{:S(2)}, u32[]{:S(2)}) %collective-permute-start.32) | collective-permute-done | bytes 524320 | tf_op jit(solution)/shard_map/ppermute | solution.py:15
  1115.7 6.4 collective-permute-done.27
  1122.9 239.2 %all-reduce.13.cloned.1.call-done = f32[2,8,256,128]{3,2,1,0:T(8,128)} async-done(((f32[2,8,256,128]{3,2,1,0:T(8,128)}), f32[2,8,256,128]{3,2,1,0:T(8,128)}) %all-reduce.13.cloned.1.call-update) | async-done | bytes 2097168 | tf_op jit(solution)/shard_map/psum | solution.py:292
  (261 shorter events, 162.5 us)
Async XLA Ops:
  7.2 366.2 %all-reduce.15.cloned.1.call-start = ((), (), s32[]{:S(2)}) async-start(), calls=%async_computation.2 | async-start | bytes 4194304 | tf_op jit(solution)/shard_map/psum | solution.py:20
  15.0 38.0 %collective-permute-start = (bf16[128,2048]{1,0:T(8,128)(2,1)}, bf16[128,2048]{1,0:T(8,128)(2,1)}, u32[]{:S(2)}, u32[]{:S(2)}) collective-permute-start(bf16[128,2048]{1,0:T(8,128)(2,1)} %get-tuple-element.53), channel_id=1, source_target_pairs={{0,2},{2,4},{4,6},{6,8},{8,10},{10,12},{12,14},{14,16},{16,18},{18... | collective-permute-start | bytes 1572872 | tf_op jit(solution)/shard_map/ppermute | solution.py:30
  20.1 33.0 %collective-permute-start.1 = (bf16[128,2048]{1,0:T(8,128)(2,1)}, bf16[128,2048]{1,0:T(8,128)(2,1)}, u32[]{:S(2)}, u32[]{:S(2)}) collective-permute-start(bf16[128,2048]{1,0:T(8,128)(2,1)} %get-tuple-element.54), channel_id=1, source_target_pairs={{2,0},{4,2},{6,4},{8,6},{10,8},{12,10},{14,12},{16,14},{18,16},{20... | collective-permute-start | bytes 1572872 | tf_op jit(solution)/shard_map/ppermute | solution.py:31
  22.3 22.2 %collective-permute-start.2 = (bf16[128,2048]{1,0:T(8,128)(2,1)}, bf16[128,2048]{1,0:T(8,128)(2,1)}, u32[]{:S(2)}, u32[]{:S(2)}) collective-permute-start(bf16[128,2048]{1,0:T(8,128)(2,1)} %get-tuple-element.55), channel_id=1, source_target_pairs={{0,2},{2,0},{4,6},{6,4},{8,10},{10,8},{12,14},{14,12},{16,18},{18,... | collective-permute-start | bytes 1572872 | tf_op jit(solution)/shard_map/ppermute | solution.py:15
  22.4 25.4 %collective-permute-start.7 = (bf16[128,2048]{1,0:T(8,128)(2,1)}, bf16[128,2048]{1,0:T(8,128)(2,1)}, u32[]{:S(2)}, u32[]{:S(2)}) collective-permute-start(bf16[128,2048]{1,0:T(8,128)(2,1)} %get-tuple-element.56), channel_id=1, source_target_pairs={{0,2},{2,0},{4,6},{6,4},{8,10},{10,8},{12,14},{14,12},{16,18},{18,... | collective-permute-start | bytes 1572872 | tf_op jit(solution)/shard_map/ppermute | solution.py:15
  22.9 26.8 %collective-permute-start.12 = (bf16[128,2048]{1,0:T(8,128)(2,1)}, bf16[128,2048]{1,0:T(8,128)(2,1)}, u32[]{:S(2)}, u32[]{:S(2)}) collective-permute-start(bf16[128,2048]{1,0:T(8,128)(2,1)} %get-tuple-element.57), channel_id=1, source_target_pairs={{0,2},{2,0},{4,6},{6,4},{8,10},{10,8},{12,14},{14,12},{16,18},{18,... | collective-permute-start | bytes 1572872 | tf_op jit(solution)/shard_map/ppermute | solution.py:15
  30.4 756.5 %all-reduce.11.cloned.1.call-start = ((), (), s32[]{:S(2)}) async-start(), calls=%async_computation | async-start | bytes 2097152 | tf_op jit(solution)/shard_map/psum | solution.py:196
  49.7 35.6 %collective-permute-start.8 = (bf16[128,2048]{1,0:T(8,128)(2,1)}, bf16[128,2048]{1,0:T(8,128)(2,1)}, u32[]{:S(2)}, u32[]{:S(2)}) collective-permute-start(bf16[128,2048]{1,0:T(8,128)(2,1)} %broadcast_select_fusion.16), channel_id=1, source_target_pairs={{0,4},{2,6},{4,0},{6,2},{8,12},{10,14},{12,8},{14,10},{16,20},{18,... | collective-permute-start | bytes 1572872 | tf_op jit(solution)/shard_map/ppermute | solution.py:15
  51.6 46.9 %collective-permute-start.13 = (bf16[128,2048]{1,0:T(8,128)(2,1)}, bf16[128,2048]{1,0:T(8,128)(2,1)}, u32[]{:S(2)}, u32[]{:S(2)}) collective-permute-start(bf16[128,2048]{1,0:T(8,128)(2,1)} %broadcast_select_fusion.12), channel_id=1, source_target_pairs={{0,4},{2,6},{4,0},{6,2},{8,12},{10,14},{12,8},{14,10},{16,20},{18,... | collective-permute-start | bytes 1572872 | tf_op jit(solution)/shard_map/ppermute | solution.py:15
  62.5 40.4 %collective-permute-start.4 = (bf16[128,2048]{1,0:T(8,128)(2,1)S(1)}, bf16[128,2048]{1,0:T(8,128)(2,1)S(1)}, u32[]{:S(2)}, u32[]{:S(2)}) collective-permute-start(bf16[128,2048]{1,0:T(8,128)(2,1)S(1)} %broadcast_select_fusion.21), channel_id=1, source_target_pairs={{0,8},{2,10},{4,12},{6,14},{8,0},{10,2},{12,4},{14,6},{16,24},{18,... | collective-permute-start | bytes 1572872 | tf_op jit(solution)/shard_map/ppermute | solution.py:15
  86.4 73.7 %collective-permute-start.9 = (bf16[128,2048]{1,0:T(8,128)(2,1)S(1)}, bf16[128,2048]{1,0:T(8,128)(2,1)S(1)}, u32[]{:S(2)}, u32[]{:S(2)}) collective-permute-start(bf16[128,2048]{1,0:T(8,128)(2,1)S(1)} %broadcast_select_fusion.17), channel_id=1, source_target_pairs={{0,8},{2,10},{4,12},{6,14},{8,0},{10,2},{12,4},{14,6},{16,24},{18,... | collective-permute-start | bytes 1572872 | tf_op jit(solution)/shard_map/ppermute | solution.py:15
  99.6 86.4 %collective-permute-start.14 = (bf16[128,2048]{1,0:T(8,128)(2,1)S(1)}, bf16[128,2048]{1,0:T(8,128)(2,1)S(1)}, u32[]{:S(2)}, u32[]{:S(2)}) collective-permute-start(bf16[128,2048]{1,0:T(8,128)(2,1)S(1)} %broadcast_select_fusion.13), channel_id=1, source_target_pairs={{0,8},{2,10},{4,12},{6,14},{8,0},{10,2},{12,4},{14,6},{16,24},{18,... | collective-permute-start | bytes 1572872 | tf_op jit(solution)/shard_map/ppermute | solution.py:15
  103.8 417.7 %collective-permute-start.5 = (bf16[128,2048]{1,0:T(8,128)(2,1)}, bf16[128,2048]{1,0:T(8,128)(2,1)}, u32[]{:S(2)}, u32[]{:S(2)}) collective-permute-start(bf16[128,2048]{1,0:T(8,128)(2,1)} %broadcast_select_fusion.22), channel_id=1, source_target_pairs={{0,16},{2,18},{4,20},{6,22},{8,24},{10,26},{12,28},{14,30},{16,0},... | collective-permute-start | bytes 1572872 | tf_op jit(solution)/shard_map/ppermute | solution.py:15
  160.9 362.1 %collective-permute-start.10 = (bf16[128,2048]{1,0:T(8,128)(2,1)}, bf16[128,2048]{1,0:T(8,128)(2,1)}, u32[]{:S(2)}, u32[]{:S(2)}) collective-permute-start(bf16[128,2048]{1,0:T(8,128)(2,1)} %broadcast_select_fusion.18), channel_id=1, source_target_pairs={{0,16},{2,18},{4,20},{6,22},{8,24},{10,26},{12,28},{14,30},{16,0},... | collective-permute-start | bytes 1572872 | tf_op jit(solution)/shard_map/ppermute | solution.py:15
  186.8 340.1 %collective-permute-start.15 = (bf16[128,2048]{1,0:T(8,128)(2,1)}, bf16[128,2048]{1,0:T(8,128)(2,1)}, u32[]{:S(2)}, u32[]{:S(2)}) collective-permute-start(bf16[128,2048]{1,0:T(8,128)(2,1)} %broadcast_select_fusion.14), channel_id=1, source_target_pairs={{0,16},{2,18},{4,20},{6,22},{8,24},{10,26},{12,28},{14,30},{16,0},... | collective-permute-start | bytes 1572872 | tf_op jit(solution)/shard_map/ppermute | solution.py:15
  521.4 840.8 %all-reduce.13.cloned.1.call-start = ((), (), s32[]{:S(2)}) async-start(), calls=%async_computation.1 | async-start | bytes 4194304 | tf_op jit(solution)/shard_map/psum | solution.py:292
  524.2 24.9 %collective-permute-start.11 = (bf16[128,2048]{1,0:T(8,128)(2,1)S(1)}, bf16[128,2048]{1,0:T(8,128)(2,1)S(1)}, u32[]{:S(2)}, u32[]{:S(2)}) collective-permute-start(bf16[128,2048]{1,0:T(8,128)(2,1)S(1)} %broadcast_select_fusion.19), channel_id=1, source_target_pairs={{0,32},{2,34},{4,36},{6,38},{8,40},{10,42},{12,44},{14,46},{16,48}... | collective-permute-start | bytes 1572872 | tf_op jit(solution)/shard_map/ppermute | solution.py:15
  528.0 33.0 %collective-permute-start.16 = (bf16[128,2048]{1,0:T(8,128)(2,1)S(1)}, bf16[128,2048]{1,0:T(8,128)(2,1)S(1)}, u32[]{:S(2)}, u32[]{:S(2)}) collective-permute-start(bf16[128,2048]{1,0:T(8,128)(2,1)S(1)} %broadcast_select_fusion.15), channel_id=1, source_target_pairs={{0,32},{2,34},{4,36},{6,38},{8,40},{10,42},{12,44},{14,46},{16,48}... | collective-permute-start | bytes 1572872 | tf_op jit(solution)/shard_map/ppermute | solution.py:15
  962.3 32.7 %collective-permute-start.17 = (bf16[2,8,128,128]{3,2,1,0:T(8,128)(2,1)}, bf16[2,8,128,128]{3,2,1,0:T(8,128)(2,1)}, u32[]{:S(2)}, u32[]{:S(2)}) collective-permute-start(bf16[2,8,128,128]{3,2,1,0:T(8,128)(2,1)} %slice.260), channel_id=1, source_target_pairs={{2,0},{4,2},{6,4},{8,6},{10,8},{12,10},{14,12},{16,14},{18,16},{20... | collective-permute-start | bytes 1572872 | tf_op jit(solution)/shard_map/ppermute | solution.py:39
  971.0 25.1 %collective-permute-start.20 = (bf16[2,8,128,128]{3,2,1,0:T(8,128)(2,1)}, bf16[2,8,128,128]{3,2,1,0:T(8,128)(2,1)}, u32[]{:S(2)}, u32[]{:S(2)}) collective-permute-start(bf16[2,8,128,128]{3,2,1,0:T(8,128)(2,1)} %get-tuple-element.43), channel_id=1, source_target_pairs={{0,4},{2,6},{4,0},{6,2},{8,12},{10,14},{12,8},{14,10},{16,20},{18,... | collective-permute-start | bytes 1572872 | tf_op jit(solution)/shard_map/ppermute | solution.py:15
  972.5 25.0 %collective-permute-start.30 = (bf16[2,8,128,128]{3,2,1,0:T(8,128)(2,1)}, bf16[2,8,128,128]{3,2,1,0:T(8,128)(2,1)}, u32[]{:S(2)}, u32[]{:S(2)}) collective-permute-start(bf16[2,8,128,128]{3,2,1,0:T(8,128)(2,1)} %get-tuple-element.44), channel_id=1, source_target_pairs={{0,4},{2,6},{4,0},{6,2},{8,12},{10,14},{12,8},{14,10},{16,20},{18,... | collective-permute-start | bytes 1572872 | tf_op jit(solution)/shard_map/ppermute | solution.py:15
  988.7 382.8 %collective-permute-start.18 = (f32[2,8,128,128]{3,2,1,0:T(8,128)}, f32[2,8,128,128]{3,2,1,0:T(8,128)}, u32[]{:S(2)}, u32[]{:S(2)}) collective-permute-start(f32[2,8,128,128]{3,2,1,0:T(8,128)} %get-tuple-element.37), channel_id=1, source_target_pairs={{0,2},{2,4},{4,6},{6,8},{8,10},{10,12},{12,14},{14,16},{16,18},{18... | collective-permute-start | bytes 3145736 | tf_op jit(solution)/shard_map/ppermute | solution.py:39
  995.0 35.8 %collective-permute-start.25 = (bf16[2,8,128,128]{3,2,1,0:T(8,128)(2,1)}, bf16[2,8,128,128]{3,2,1,0:T(8,128)(2,1)S(1)}, u32[]{:S(2)}, u32[]{:S(2)}) collective-permute-start(bf16[2,8,128,128]{3,2,1,0:T(8,128)(2,1)} %get-tuple-element.45), channel_id=1, source_target_pairs={{0,4},{2,6},{4,0},{6,2},{8,12},{10,14},{12,8},{14,10},{16,20},{18,... | collective-permute-start | bytes 1572872 | tf_op jit(solution)/shard_map/ppermute | solution.py:15
  997.3 50.0 %collective-permute-start.21 = (bf16[2,8,128,128]{3,2,1,0:T(8,128)(2,1)S(1)}, bf16[2,8,128,128]{3,2,1,0:T(8,128)(2,1)S(1)}, u32[]{:S(2)}, u32[]{:S(2)}) collective-permute-start(bf16[2,8,128,128]{3,2,1,0:T(8,128)(2,1)S(1)} %broadcast_select_fusion.9), channel_id=1, source_target_pairs={{0,8},{2,10},{4,12},{6,14},{8,0},{10,2},{12,4},{14,6},{16,24},{18,... | collective-permute-start | bytes 1572872 | tf_op jit(solution)/shard_map/ppermute | solution.py:15
  998.7 66.7 %collective-permute-start.31 = (bf16[2,8,128,128]{3,2,1,0:T(8,128)(2,1)S(1)}, bf16[2,8,128,128]{3,2,1,0:T(8,128)(2,1)S(1)}, u32[]{:S(2)}, u32[]{:S(2)}) collective-permute-start(bf16[2,8,128,128]{3,2,1,0:T(8,128)(2,1)S(1)} %broadcast_select_fusion.1), channel_id=1, source_target_pairs={{0,8},{2,10},{4,12},{6,14},{8,0},{10,2},{12,4},{14,6},{16,24},{18,... | collective-permute-start | bytes 1572872 | tf_op jit(solution)/shard_map/ppermute | solution.py:15
  1031.9 49.1 %collective-permute-start.26 = (bf16[2,8,128,128]{3,2,1,0:T(8,128)(2,1)S(1)}, bf16[2,8,128,128]{3,2,1,0:T(8,128)(2,1)S(1)}, u32[]{:S(2)}, u32[]{:S(2)}) collective-permute-start(bf16[2,8,128,128]{3,2,1,0:T(8,128)(2,1)S(1)} %broadcast_select_fusion.5), channel_id=1, source_target_pairs={{0,8},{2,10},{4,12},{6,14},{8,0},{10,2},{12,4},{14,6},{16,24},{18,... | collective-permute-start | bytes 1572872 | tf_op jit(solution)/shard_map/ppermute | solution.py:15
  1047.3 46.0 %collective-permute-start.22 = (bf16[2,8,128,128]{3,2,1,0:T(8,128)(2,1)S(1)}, bf16[2,8,128,128]{3,2,1,0:T(8,128)(2,1)S(1)}, u32[]{:S(2)}, u32[]{:S(2)}) collective-permute-start(bf16[2,8,128,128]{3,2,1,0:T(8,128)(2,1)S(1)} %broadcast_select_fusion.10), channel_id=1, source_target_pairs={{0,16},{2,18},{4,20},{6,22},{8,24},{10,26},{12,28},{14,30},{16,0},... | collective-permute-start | bytes 1572872 | tf_op jit(solution)/shard_map/ppermute | solution.py:15
  1065.4 49.4 %collective-permute-start.32 = (bf16[2,8,128,128]{3,2,1,0:T(8,128)(2,1)S(1)}, bf16[2,8,128,128]{3,2,1,0:T(8,128)(2,1)S(1)}, u32[]{:S(2)}, u32[]{:S(2)}) collective-permute-start(bf16[2,8,128,128]{3,2,1,0:T(8,128)(2,1)S(1)} %broadcast_select_fusion.2), channel_id=1, source_target_pairs={{0,16},{2,18},{4,20},{6,22},{8,24},{10,26},{12,28},{14,30},{16,0},... | collective-permute-start | bytes 1572872 | tf_op jit(solution)/shard_map/ppermute | solution.py:15
  1081.0 41.0 %collective-permute-start.27 = (bf16[2,8,128,128]{3,2,1,0:T(8,128)(2,1)S(1)}, bf16[2,8,128,128]{3,2,1,0:T(8,128)(2,1)S(1)}, u32[]{:S(2)}, u32[]{:S(2)}) collective-permute-start(bf16[2,8,128,128]{3,2,1,0:T(8,128)(2,1)S(1)} %broadcast_select_fusion.6), channel_id=1, source_target_pairs={{0,16},{2,18},{4,20},{6,22},{8,24},{10,26},{12,28},{14,30},{16,0},... | collective-permute-start | bytes 1572872 | tf_op jit(solution)/shard_map/ppermute | solution.py:15
  1093.3 268.9 %collective-permute-start.23 = (bf16[2,8,128,128]{3,2,1,0:T(8,128)(2,1)S(1)}, bf16[2,8,128,128]{3,2,1,0:T(8,128)(2,1)}, u32[]{:S(2)}, u32[]{:S(2)}) collective-permute-start(bf16[2,8,128,128]{3,2,1,0:T(8,128)(2,1)S(1)} %broadcast_select_fusion.11), channel_id=1, source_target_pairs={{0,32},{2,34},{4,36},{6,38},{8,40},{10,42},{12,44},{14,46},{16,48}... | collective-permute-start | bytes 1572872 | tf_op jit(solution)/shard_map/ppermute | solution.py:15
  1115.7 247.5 %collective-permute-start.33 = (bf16[2,8,128,128]{3,2,1,0:T(8,128)(2,1)}, bf16[2,8,128,128]{3,2,1,0:T(8,128)(2,1)}, u32[]{:S(2)}, u32[]{:S(2)}) collective-permute-start(bf16[2,8,128,128]{3,2,1,0:T(8,128)(2,1)} %broadcast_select_fusion.3), channel_id=1, source_target_pairs={{0,32},{2,34},{4,36},{6,38},{8,40},{10,42},{12,44},{14,46},{16,48}... | collective-permute-start | bytes 1572872 | tf_op jit(solution)/shard_map/ppermute | solution.py:15
  1122.9 242.4 %collective-permute-start.28 = (bf16[2,8,128,128]{3,2,1,0:T(8,128)(2,1)}, bf16[2,8,128,128]{3,2,1,0:T(8,128)(2,1)}, u32[]{:S(2)}, u32[]{:S(2)}) collective-permute-start(bf16[2,8,128,128]{3,2,1,0:T(8,128)(2,1)} %broadcast_select_fusion.7), channel_id=1, source_target_pairs={{0,32},{2,34},{4,36},{6,38},{8,40},{10,42},{12,44},{14,46},{16,48}... | collective-permute-start | bytes 1572872 | tf_op jit(solution)/shard_map/ppermute | solution.py:15
  (45 other events, 2048.0 us)
Sparse Core Ops, SparseCore 0:
  30.5 342.8 all-reduce.14
  521.5 265.3 all-reduce.10
  988.8 373.3 all-reduce.12
